TPU v7x, 256 devices: a whole 4x4x8 slice. The times are simulated.
256 devices in a mesh: rows: 16 (over x, y_lo, core), cols: 16 (over z, y_hi).
Axes of the slice: x: 4, y: 4 (y_hi: 2, y_lo: 2; y = y_hi * 2 + y_lo), z: 8, core: 2. Of those that a mesh axis runs over, the one named last changes fastest.
Arguments:
- unary: float32 [21, 256, 2048], P(None, 'rows', 'cols'), may hold values from -8 to 300
- features: bfloat16 [64, 256, 2048], P(None, 'rows', 'cols'), may hold values from -9 to 9
- compat: float32 [21, 21], replicated, may hold values from -6 to 6
- grad_output: float32 [21, 256, 2048], P(None, 'rows', 'cols'), may hold values from -6 to 6
Outputs:
- unary_grad: float32 [21, 256, 2048], P(None, 'rows', 'cols')
- feature_grad: float32 [64, 256, 2048], P(None, 'rows', 'cols')
- compat_grad: float32 [21, 21], replicated
All inputs are finite; a program needn't handle non-finite values.
Results may differ from a plain program's by a relative error of at most 0.0003.
Values may be sent and summed in bfloat16 or wider, within the bound.
A program may use at most 128 MiB of HBM per device.

v0:
```python
import math
import jax
import jax.numpy as jnp
from jax import lax
from jax.sharding import PartitionSpec as P

ITERS = 2
THETA_PIXELS = 3.0
WINDOW_OFFSETS = [
    (row_step, col_step)
    for row_step in range(-3, 4)
    for col_step in range(-3, 4)
    if row_step != 0 or col_step != 0
]


def with_halo(block, sides, width):
    for axis, dim in sides:
        count = lax.axis_size(axis)
        forward = [(i, i + 1) for i in range(count - 1)]
        backward = [(target, source) for source, target in forward]
        low = lax.ppermute(
            lax.slice_in_dim(block, block.shape[dim] - width, None, axis=dim), axis, forward
        )
        high = lax.ppermute(lax.slice_in_dim(block, 0, width, axis=dim), axis, backward)
        block = jnp.concatenate([low, block, high], axis=dim)
    return block


def spatial_weight(row_step, col_step):
    return math.exp(
        -(row_step * row_step + col_step * col_step) / (2.0 * THETA_PIXELS * THETA_PIXELS)
    )


def shifted_view(padded, row_step, col_step, height, width_cells):
    return padded[
        :, 3 + row_step : 3 + row_step + height, 3 + col_step : 3 + col_step + width_cells
    ]


def affinity(padded_features):
    height = padded_features.shape[1] - 6
    width_cells = padded_features.shape[2] - 6
    center = shifted_view(padded_features, 0, 0, height, width_cells).astype(jnp.float32)
    factor = 1.0 / (2.0 * padded_features.shape[0])
    layers = []
    for row_step, col_step in WINDOW_OFFSETS:
        shifted = shifted_view(padded_features, row_step, col_step, height, width_cells).astype(
            jnp.float32
        )
        distance = jnp.sum((shifted - center) * (shifted - center), axis=0)
        layers.append(spatial_weight(row_step, col_step) * jnp.exp(-distance * factor))
    return jnp.stack(layers)


def message(kernel, padded):
    height = kernel.shape[1]
    width_cells = kernel.shape[2]
    total = jnp.zeros((padded.shape[0], height, width_cells), jnp.float32)
    for number, (row_step, col_step) in enumerate(WINDOW_OFFSETS):
        total = total + kernel[number][None] * shifted_view(
            padded, row_step, col_step, height, width_cells
        )
    return total


def pair_terms(grad_padded, prob_padded):
    height = grad_padded.shape[1] - 6
    width_cells = grad_padded.shape[2] - 6
    grad_center = shifted_view(grad_padded, 0, 0, height, width_cells)
    prob_center = shifted_view(prob_padded, 0, 0, height, width_cells)
    layers = []
    for row_step, col_step in WINDOW_OFFSETS:
        prob_shift = shifted_view(prob_padded, row_step, col_step, height, width_cells)
        grad_shift = shifted_view(grad_padded, row_step, col_step, height, width_cells)
        layers.append(jnp.sum(grad_center * prob_shift + grad_shift * prob_center, axis=0))
    return jnp.stack(layers)


def feature_term(coefs, kernel, padded_features):
    height = kernel.shape[1]
    width_cells = kernel.shape[2]
    center = shifted_view(padded_features, 0, 0, height, width_cells).astype(jnp.float32)
    factor = 1.0 / padded_features.shape[0]
    total = jnp.zeros(center.shape, jnp.float32)
    for number, (row_step, col_step) in enumerate(WINDOW_OFFSETS):
        shifted = shifted_view(padded_features, row_step, col_step, height, width_cells).astype(
            jnp.float32
        )
        weight_map = coefs[number] * kernel[number] * factor
        total = total + weight_map[None] * (shifted - center)
    return total


def mix(compat, values):
    return jnp.einsum("cd,dhw->chw", compat, values, precision=lax.Precision.HIGHEST)


def mix_back(compat, values):
    return jnp.einsum("cd,chw->dhw", compat, values, precision=lax.Precision.HIGHEST)


def outer_sum(left, right):
    return jnp.einsum("chw,dhw->cd", left, right, precision=lax.Precision.HIGHEST)


def softmax_grad(prob, cotangent):
    return prob * (cotangent - jnp.sum(cotangent * prob, axis=0, keepdims=True))


def on_device(unary, features, compat, grad_output):
    height = unary.shape[1]
    width_cells = unary.shape[2]
    total_pixels = height * lax.axis_size("rows") * width_cells * lax.axis_size("cols")
    reach = 0
    feat_wide = with_halo(features, (("rows", 1), ("cols", 2)), 3)
    cotangent = grad_output
    start_prob = jax.nn.softmax(unary, axis=0)
    kern_store = affinity(feat_wide)

    def kernel_at():
        return kern_store

    prob_list = [start_prob]
    pad_list = [reach]
    wide_list = []
    message_list = []
    for step in range(ITERS):
        current = prob_list[-1]
        prob_wide = with_halo(current, (("rows", 1), ("cols", 2)), 3)
        wide_pad = 3
        wide_list.append((prob_wide, wide_pad))
        out_pad = wide_pad - 3
        message_out = message(kernel_at(), prob_wide)
        message_list.append(message_out)
        logits = unary - mix(compat, message_out)
        next_prob = jax.nn.softmax(logits, axis=0)
        prob_list.append(next_prob)
        pad_list.append(out_pad)
    unary_sum = jnp.zeros(unary.shape, jnp.float32)
    compat_sum = jnp.zeros(compat.shape, jnp.float32)
    coefs = jnp.zeros((len(WINDOW_OFFSETS), height, width_cells), jnp.float32)
    for step in reversed(range(ITERS)):
        later_prob = prob_list[step + 1]
        logit_grad = softmax_grad(later_prob, cotangent)
        unary_sum = unary_sum + logit_grad
        compat_sum = compat_sum - outer_sum(logit_grad, message_list[step])
        msg_grad = -mix_back(compat, logit_grad)
        grad_wide = with_halo(msg_grad, (("rows", 1), ("cols", 2)), 3)
        cotangent = message(kernel_at(), grad_wide)
        prob_wide, wide_pad = wide_list[step]
        coefs = coefs + pair_terms(grad_wide, prob_wide)
    unary_grad = unary_sum + softmax_grad(prob_list[0], cotangent)
    feature_grad = feature_term(coefs, kernel_at(), feat_wide)
    compat_grad = lax.psum(compat_sum, ("rows", "cols")) / math.sqrt(total_pixels)
    return (unary_grad, feature_grad, compat_grad)


def solution(mesh):
    placed = (P(None, "rows", "cols"), P(None, "rows", "cols"), P(), P(None, "rows", "cols"))
    return jax.shard_map(
        on_device,
        mesh=mesh,
        in_specs=placed,
        out_specs=(P(None, "rows", "cols"), P(None, "rows", "cols"), P()),
        check_vma=False,
    )
```

profile of v0, /device:TPU:33, one launch (start us, length us, event | category | flops | bytes accessed | tf_op | source)
XLA Modules:
  0.0 314.2 jit_solution(16345287022579159694)
XLA Ops:
  3.7 3.8 %collective-permute-start.3 = (f32[21,3,128]{2,0,1:T(8,128)S(1)}, f32[21,3,128]{2,0,1:T(8,128)S(1)}, u32[]{:S(2)}, u32[]{:S(2)}) collective-permute-start(f32[21,3,128]{2,0,1:T(8,128)S(1)} %get-tuple-element.238), channel_id=1, source_target_pairs={{0,16},{16,32},{32,48},{48,64},{64,80},{80,96},{96,112},{112,128},... | collective-permute-start | bytes 96776 | tf_op jit(solution)/shard_map/ppermute | solution.py:22
  9.5 3.6 %collective-permute-start = (bf16[64,3,128]{2,1,0:T(4,128)(2,1)S(1)}, bf16[64,3,128]{2,1,0:T(4,128)(2,1)S(1)}, u32[]{:S(2)}, u32[]{:S(2)}) collective-permute-start(bf16[64,3,128]{2,1,0:T(4,128)(2,1)S(1)} %get-tuple-element.229), channel_id=1, source_target_pairs={{0,16},{16,32},{32,48},{48,64},{64,80},{80,96},{96,112},{112,128},... | collective-permute-start | bytes 147464 | tf_op jit(solution)/shard_map/ppermute | solution.py:22
  15.2 4.5 %collective-permute-start.5 = (f32[21,22,3]{2,0,1:T(8,128)S(1)}, f32[21,22,3]{2,0,1:T(8,128)S(1)}, u32[]{:S(2)}, u32[]{:S(2)}) collective-permute-start(f32[21,22,3]{2,0,1:T(8,128)S(1)} %get-tuple-element.227), channel_id=1, source_target_pairs={{0,1},{1,2},{2,3},{3,4},{4,5},{5,6},{6,7},{7,8},{8,9},{9,10},{10,1... | collective-permute-start | bytes 16640 | tf_op jit(solution)/shard_map/ppermute | solution.py:22
  19.8 3.2 %collective-permute-start.7 = (f32[21,22,3]{2,0,1:T(8,128)S(1)}, f32[21,22,3]{2,0,1:T(8,128)S(1)}, u32[]{:S(2)}, u32[]{:S(2)}) collective-permute-start(f32[21,22,3]{2,0,1:T(8,128)S(1)} %get-tuple-element.228), channel_id=1, source_target_pairs={{1,0},{2,1},{3,2},{4,3},{5,4},{6,5},{7,6},{8,7},{9,8},{10,9},{11,1... | collective-permute-start | bytes 16640 | tf_op jit(solution)/shard_map/ppermute | solution.py:25
  23.0 8.2 %collective-permute-done.5 = f32[21,22,3]{2,0,1:T(8,128)S(1)} collective-permute-done((f32[21,22,3]{2,0,1:T(8,128)S(1)}, f32[21,22,3]{2,0,1:T(8,128)S(1)}, u32[]{:S(2)}, u32[]{:S(2)}) %collective-permute-start.5) | collective-permute-done | bytes 5576 | tf_op jit(solution)/shard_map/ppermute | solution.py:22
  36.7 3.8 %collective-permute-start.2 = (bf16[64,22,3]{2,1,0:T(8,128)(2,1)S(1)}, bf16[64,22,3]{2,1,0:T(8,128)(2,1)S(1)}, u32[]{:S(2)}, u32[]{:S(2)}) collective-permute-start(bf16[64,22,3]{2,1,0:T(8,128)(2,1)S(1)} %get-tuple-element.212), channel_id=1, source_target_pairs={{0,1},{1,2},{2,3},{3,4},{4,5},{5,6},{6,7},{7,8},{8,9},{9,10},{10,1... | collective-permute-start | bytes 25352 | tf_op jit(solution)/shard_map/ppermute | solution.py:22
  40.5 15.3 %collective-permute-done.6 = bf16[64,22,3]{2,1,0:T(8,128)(2,1)S(1)} collective-permute-done((bf16[64,22,3]{2,1,0:T(8,128)(2,1)S(1)}, bf16[64,22,3]{2,1,0:T(8,128)(2,1)S(1)}, u32[]{:S(2)}, u32[]{:S(2)}) %collective-permute-start.6) | collective-permute-done | bytes 8480 | tf_op jit(solution)/shard_map/ppermute | solution.py:25
  83.4 5.8 %collective-permute-start.8 = (f32[21,3,128]{2,0,1:T(8,128)S(1)}, f32[21,3,128]{2,0,1:T(8,128)S(1)}, u32[]{:S(2)}, u32[]{:S(2)}) collective-permute-start(f32[21,3,128]{2,0,1:T(8,128)S(1)} %get-tuple-element.236), channel_id=1, source_target_pairs={{0,16},{16,32},{32,48},{48,64},{64,80},{80,96},{96,112},{112,128},... | collective-permute-start | bytes 96776 | tf_op jit(solution)/shard_map/ppermute | solution.py:22
  91.1 3.3 %collective-permute-done.9 = f32[21,3,128]{2,0,1:T(8,128)S(1)} collective-permute-done((f32[21,3,128]{2,0,1:T(8,128)S(1)}, f32[21,3,128]{2,0,1:T(8,128)S(1)}, u32[]{:S(2)}, u32[]{:S(2)}) %collective-permute-start.9) | collective-permute-done | bytes 32288 | tf_op jit(solution)/shard_map/ppermute | solution.py:25
  94.6 4.8 %collective-permute-start.10 = (f32[21,22,3]{2,0,1:T(8,128)S(1)}, f32[21,22,3]{2,0,1:T(8,128)S(1)}, u32[]{:S(2)}, u32[]{:S(2)}) collective-permute-start(f32[21,22,3]{2,0,1:T(8,128)S(1)} %get-tuple-element.223), channel_id=1, source_target_pairs={{0,1},{1,2},{2,3},{3,4},{4,5},{5,6},{6,7},{7,8},{8,9},{9,10},{10,1... | collective-permute-start | bytes 16640 | tf_op jit(solution)/shard_map/ppermute | solution.py:22
  102.5 7.3 %collective-permute-done.10 = f32[21,22,3]{2,0,1:T(8,128)S(1)} collective-permute-done((f32[21,22,3]{2,0,1:T(8,128)S(1)}, f32[21,22,3]{2,0,1:T(8,128)S(1)}, u32[]{:S(2)}, u32[]{:S(2)}) %collective-permute-start.10) | collective-permute-done | bytes 5576 | tf_op jit(solution)/shard_map/ppermute | solution.py:22
  118.5 4.6 %collective-permute-start.12 = (f32[21,3,128]{2,0,1:T(8,128)S(1)}, f32[21,3,128]{2,0,1:T(8,128)S(1)}, u32[]{:S(2)}, u32[]{:S(2)}) collective-permute-start(f32[21,3,128]{2,0,1:T(8,128)S(1)} %get-tuple-element.234), channel_id=1, source_target_pairs={{0,16},{16,32},{32,48},{48,64},{64,80},{80,96},{96,112},{112,128},... | collective-permute-start | bytes 96776 | tf_op jit(solution)/shard_map/ppermute | solution.py:22
  125.0 3.3 %collective-permute-done.13 = f32[21,3,128]{2,0,1:T(8,128)S(1)} collective-permute-done((f32[21,3,128]{2,0,1:T(8,128)S(1)}, f32[21,3,128]{2,0,1:T(8,128)S(1)}, u32[]{:S(2)}, u32[]{:S(2)}) %collective-permute-start.13) | collective-permute-done | bytes 32288 | tf_op jit(solution)/shard_map/ppermute | solution.py:25
  128.5 3.9 %collective-permute-start.14 = (f32[21,22,3]{2,0,1:T(8,128)S(1)}, f32[21,22,3]{2,0,1:T(8,128)S(1)}, u32[]{:S(2)}, u32[]{:S(2)}) collective-permute-start(f32[21,22,3]{2,0,1:T(8,128)S(1)} %get-tuple-element.219), channel_id=1, source_target_pairs={{0,1},{1,2},{2,3},{3,4},{4,5},{5,6},{6,7},{7,8},{8,9},{9,10},{10,1... | collective-permute-start | bytes 16640 | tf_op jit(solution)/shard_map/ppermute | solution.py:22
  132.4 3.8 %collective-permute-start.15 = (f32[21,22,3]{2,0,1:T(8,128)S(1)}, f32[21,22,3]{2,0,1:T(8,128)S(1)}, u32[]{:S(2)}, u32[]{:S(2)}) collective-permute-start(f32[21,22,3]{2,0,1:T(8,128)S(1)} %get-tuple-element.220), channel_id=1, source_target_pairs={{1,0},{2,1},{3,2},{4,3},{5,4},{6,5},{7,6},{8,7},{9,8},{10,9},{11,1... | collective-permute-start | bytes 16640 | tf_op jit(solution)/shard_map/ppermute | solution.py:25
  136.9 5.8 %collective-permute-done.14 = f32[21,22,3]{2,0,1:T(8,128)S(1)} collective-permute-done((f32[21,22,3]{2,0,1:T(8,128)S(1)}, f32[21,22,3]{2,0,1:T(8,128)S(1)}, u32[]{:S(2)}, u32[]{:S(2)}) %collective-permute-start.14) | collective-permute-done | bytes 5576 | tf_op jit(solution)/shard_map/ppermute | solution.py:22
  152.1 4.4 %add_reduce_fusion.48 = (f32[16,128]{1,0:T(8,128)}, f32[16,128]{1,0:T(8,128)}, f32[16,128]{1,0:T(8,128)}, f32[16,128]{1,0:T(8,128)}, f32[16,128]{1,0:T(8,128)}, ...) fusion(f32[21,16,128]{2,0,1:T(8,128)S(1)} %fusion.11, ...), kind=kLoop, calls=%fused_computation.349 | loop fusion | flops 5830656 | bytes 9657344 | tf_op jit(solution)/shard_map/reduce_sum | solution.py:77
  159.8 81.1 %psum.7 = f32[21,21]{1,0:T(8,128)S(1)} all-reduce(f32[21,21]{1,0:T(8,128)S(1)} %fusion.15), channel_id=1, replica_groups=mesh['rows'=16,'cols'=16] {'rows','cols'}, use_global_device_ids=true, to_apply=%region_153.0 | all-reduce | flops 441 | bytes 3528 | tf_op jit(solution)/shard_map/psum | solution.py:156
  257.8 3.8 %collective-permute-start.18 = (f32[21,22,3]{2,0,1:T(8,128)S(1)}, f32[21,22,3]{2,0,1:T(8,128)S(1)}, u32[]{:S(2)}, u32[]{:S(2)}) collective-permute-start(f32[21,22,3]{2,0,1:T(8,128)S(1)} %get-tuple-element.215), channel_id=1, source_target_pairs={{0,1},{1,2},{2,3},{3,4},{4,5},{5,6},{6,7},{7,8},{8,9},{9,10},{10,1... | collective-permute-start | bytes 16640 | tf_op jit(solution)/shard_map/ppermute | solution.py:22
  261.6 4.1 %collective-permute-start.19 = (f32[21,22,3]{2,0,1:T(8,128)S(1)}, f32[21,22,3]{2,0,1:T(8,128)S(1)}, u32[]{:S(2)}, u32[]{:S(2)}) collective-permute-start(f32[21,22,3]{2,0,1:T(8,128)S(1)} %get-tuple-element.216), channel_id=1, source_target_pairs={{1,0},{2,1},{3,2},{4,3},{5,4},{6,5},{7,6},{8,7},{9,8},{10,9},{11,1... | collective-permute-start | bytes 16640 | tf_op jit(solution)/shard_map/ppermute | solution.py:25
  266.0 6.7 %collective-permute-done.18 = f32[21,22,3]{2,0,1:T(8,128)S(1)} collective-permute-done((f32[21,22,3]{2,0,1:T(8,128)S(1)}, f32[21,22,3]{2,0,1:T(8,128)S(1)}, u32[]{:S(2)}, u32[]{:S(2)}) %collective-permute-start.18) | collective-permute-done | bytes 5576 | tf_op jit(solution)/shard_map/ppermute | solution.py:22
  272.7 3.5 %collective-permute-done.19 = f32[21,22,3]{2,0,1:T(8,128)S(1)} collective-permute-done((f32[21,22,3]{2,0,1:T(8,128)S(1)}, f32[21,22,3]{2,0,1:T(8,128)S(1)}, u32[]{:S(2)}, u32[]{:S(2)}) %collective-permute-start.19) | collective-permute-done | bytes 5576 | tf_op jit(solution)/shard_map/ppermute | solution.py:25
  290.9 13.9 %fusion.7 = f32[21,16,128]{2,0,1:T(8,128)S(1)} fusion(f32[21,16,128]{2,0,1:T(8,128)S(1)} %copy-done.10, f32[16,128]{1,0:T(8,128)} %fusion.19, f32[21,16,128]{2,1,0:T(8,128)} %param.7, f32[21,16,128]{2,0,1:T(8,128)} %copy-done.11, f32[16,128]{1,0:T(8,128)} %get-tuple-element.242, f32[16,128]{1,0:T(8,128)S(1)} %copy-done.13, f32[16,128]{1,0:T(8,128)S(1)} %reduce_max.27, ...), kind=kOutput, calls=%fused_computation.55 | output fusion | flops 9205780 | bytes 18972672 | tf_op jit(solution)/shard_map/sub | solution.py:109
  305.9 8.3 %multiply_add_fusion = f32[64,16,128]{2,1,0:T(8,128)} fusion(bf16[64,16,128]{2,1,0:T(8,128)(2,1)S(1)} %copy-done.6, bf16[64,3,128]{2,1,0:T(4,128)(2,1)S(1)} %collective-permute-done, f32[16,128]{1,0:T(8,128)} %get-tuple-element.162, f32[16,128]{1,0:T(8,128)} %get-tuple-element.163, f32[16,128]{1,0:T(8,128)} %get-tuple-element.164, ...), kind=kLoop, calls=%fused_computation.80 | loop fusion | flops 26345472 | bytes 13025280 | tf_op jit(solution)/shard_map/add | solution.py:92
  (516 shorter events, 99.3 us)
Async XLA Ops:
  3.7 11.4 %collective-permute-start.3 = (f32[21,3,128]{2,0,1:T(8,128)S(1)}, f32[21,3,128]{2,0,1:T(8,128)S(1)}, u32[]{:S(2)}, u32[]{:S(2)}) collective-permute-start(f32[21,3,128]{2,0,1:T(8,128)S(1)} %get-tuple-element.238), channel_id=1, source_target_pairs={{0,16},{16,32},{32,48},{48,64},{64,80},{80,96},{96,112},{112,128},... | collective-permute-start | bytes 96776 | tf_op jit(solution)/shard_map/ppermute | solution.py:22
  7.5 7.6 %collective-permute-start.4 = (f32[21,3,128]{2,0,1:T(8,128)S(1)}, f32[21,3,128]{2,0,1:T(8,128)S(1)}, u32[]{:S(2)}, u32[]{:S(2)}) collective-permute-start(f32[21,3,128]{2,0,1:T(8,128)S(1)} %get-tuple-element.239), channel_id=1, source_target_pairs={{16,0},{32,16},{48,32},{64,48},{80,64},{96,80},{112,96},{128,112},... | collective-permute-start | bytes 96776 | tf_op jit(solution)/shard_map/ppermute | solution.py:25
  9.5 23.8 %collective-permute-start = (bf16[64,3,128]{2,1,0:T(4,128)(2,1)S(1)}, bf16[64,3,128]{2,1,0:T(4,128)(2,1)S(1)}, u32[]{:S(2)}, u32[]{:S(2)}) collective-permute-start(bf16[64,3,128]{2,1,0:T(4,128)(2,1)S(1)} %get-tuple-element.229), channel_id=1, source_target_pairs={{0,16},{16,32},{32,48},{48,64},{64,80},{80,96},{96,112},{112,128},... | collective-permute-start | bytes 147464 | tf_op jit(solution)/shard_map/ppermute | solution.py:22
  13.1 20.1 %collective-permute-start.1 = (bf16[64,3,128]{2,1,0:T(4,128)(2,1)S(1)}, bf16[64,3,128]{2,1,0:T(4,128)(2,1)S(1)}, u32[]{:S(2)}, u32[]{:S(2)}) collective-permute-start(bf16[64,3,128]{2,1,0:T(4,128)(2,1)S(1)} %get-tuple-element.230), channel_id=1, source_target_pairs={{16,0},{32,16},{48,32},{64,48},{80,64},{96,80},{112,96},{128,112},... | collective-permute-start | bytes 147464 | tf_op jit(solution)/shard_map/ppermute | solution.py:25
  15.2 15.9 %collective-permute-start.5 = (f32[21,22,3]{2,0,1:T(8,128)S(1)}, f32[21,22,3]{2,0,1:T(8,128)S(1)}, u32[]{:S(2)}, u32[]{:S(2)}) collective-permute-start(f32[21,22,3]{2,0,1:T(8,128)S(1)} %get-tuple-element.227), channel_id=1, source_target_pairs={{0,1},{1,2},{2,3},{3,4},{4,5},{5,6},{6,7},{7,8},{8,9},{9,10},{10,1... | collective-permute-start | bytes 16640 | tf_op jit(solution)/shard_map/ppermute | solution.py:22
  19.8 13.3 %collective-permute-start.7 = (f32[21,22,3]{2,0,1:T(8,128)S(1)}, f32[21,22,3]{2,0,1:T(8,128)S(1)}, u32[]{:S(2)}, u32[]{:S(2)}) collective-permute-start(f32[21,22,3]{2,0,1:T(8,128)S(1)} %get-tuple-element.228), channel_id=1, source_target_pairs={{1,0},{2,1},{3,2},{4,3},{5,4},{6,5},{7,6},{8,7},{9,8},{10,9},{11,1... | collective-permute-start | bytes 16640 | tf_op jit(solution)/shard_map/ppermute | solution.py:25
  33.7 22.1 %collective-permute-start.6 = (bf16[64,22,3]{2,1,0:T(8,128)(2,1)S(1)}, bf16[64,22,3]{2,1,0:T(8,128)(2,1)S(1)}, u32[]{:S(2)}, u32[]{:S(2)}) collective-permute-start(bf16[64,22,3]{2,1,0:T(8,128)(2,1)S(1)} %get-tuple-element.211), channel_id=1, source_target_pairs={{1,0},{2,1},{3,2},{4,3},{5,4},{6,5},{7,6},{8,7},{9,8},{10,9},{11,1... | collective-permute-start | bytes 25352 | tf_op jit(solution)/shard_map/ppermute | solution.py:25
  36.7 19.1 %collective-permute-start.2 = (bf16[64,22,3]{2,1,0:T(8,128)(2,1)S(1)}, bf16[64,22,3]{2,1,0:T(8,128)(2,1)S(1)}, u32[]{:S(2)}, u32[]{:S(2)}) collective-permute-start(bf16[64,22,3]{2,1,0:T(8,128)(2,1)S(1)} %get-tuple-element.212), channel_id=1, source_target_pairs={{0,1},{1,2},{2,3},{3,4},{4,5},{5,6},{6,7},{7,8},{8,9},{9,10},{10,1... | collective-permute-start | bytes 25352 | tf_op jit(solution)/shard_map/ppermute | solution.py:22
  83.4 7.7 %collective-permute-start.8 = (f32[21,3,128]{2,0,1:T(8,128)S(1)}, f32[21,3,128]{2,0,1:T(8,128)S(1)}, u32[]{:S(2)}, u32[]{:S(2)}) collective-permute-start(f32[21,3,128]{2,0,1:T(8,128)S(1)} %get-tuple-element.236), channel_id=1, source_target_pairs={{0,16},{16,32},{32,48},{48,64},{64,80},{80,96},{96,112},{112,128},... | collective-permute-start | bytes 96776 | tf_op jit(solution)/shard_map/ppermute | solution.py:22
  89.2 5.3 %collective-permute-start.9 = (f32[21,3,128]{2,0,1:T(8,128)S(1)}, f32[21,3,128]{2,0,1:T(8,128)S(1)}, u32[]{:S(2)}, u32[]{:S(2)}) collective-permute-start(f32[21,3,128]{2,0,1:T(8,128)S(1)} %get-tuple-element.237), channel_id=1, source_target_pairs={{16,0},{32,16},{48,32},{64,48},{80,64},{96,80},{112,96},{128,112},... | collective-permute-start | bytes 96776 | tf_op jit(solution)/shard_map/ppermute | solution.py:25
  94.6 15.2 %collective-permute-start.10 = (f32[21,22,3]{2,0,1:T(8,128)S(1)}, f32[21,22,3]{2,0,1:T(8,128)S(1)}, u32[]{:S(2)}, u32[]{:S(2)}) collective-permute-start(f32[21,22,3]{2,0,1:T(8,128)S(1)} %get-tuple-element.223), channel_id=1, source_target_pairs={{0,1},{1,2},{2,3},{3,4},{4,5},{5,6},{6,7},{7,8},{8,9},{9,10},{10,1... | collective-permute-start | bytes 16640 | tf_op jit(solution)/shard_map/ppermute | solution.py:22
  99.4 12.0 %collective-permute-start.11 = (f32[21,22,3]{2,0,1:T(8,128)S(1)}, f32[21,22,3]{2,0,1:T(8,128)S(1)}, u32[]{:S(2)}, u32[]{:S(2)}) collective-permute-start(f32[21,22,3]{2,0,1:T(8,128)S(1)} %get-tuple-element.224), channel_id=1, source_target_pairs={{1,0},{2,1},{3,2},{4,3},{5,4},{6,5},{7,6},{8,7},{9,8},{10,9},{11,1... | collective-permute-start | bytes 16640 | tf_op jit(solution)/shard_map/ppermute | solution.py:25
  118.5 6.5 %collective-permute-start.12 = (f32[21,3,128]{2,0,1:T(8,128)S(1)}, f32[21,3,128]{2,0,1:T(8,128)S(1)}, u32[]{:S(2)}, u32[]{:S(2)}) collective-permute-start(f32[21,3,128]{2,0,1:T(8,128)S(1)} %get-tuple-element.234), channel_id=1, source_target_pairs={{0,16},{16,32},{32,48},{48,64},{64,80},{80,96},{96,112},{112,128},... | collective-permute-start | bytes 96776 | tf_op jit(solution)/shard_map/ppermute | solution.py:22
  123.0 5.3 %collective-permute-start.13 = (f32[21,3,128]{2,0,1:T(8,128)S(1)}, f32[21,3,128]{2,0,1:T(8,128)S(1)}, u32[]{:S(2)}, u32[]{:S(2)}) collective-permute-start(f32[21,3,128]{2,0,1:T(8,128)S(1)} %get-tuple-element.235), channel_id=1, source_target_pairs={{16,0},{32,16},{48,32},{64,48},{80,64},{96,80},{112,96},{128,112},... | collective-permute-start | bytes 96776 | tf_op jit(solution)/shard_map/ppermute | solution.py:25
  128.5 14.3 %collective-permute-start.14 = (f32[21,22,3]{2,0,1:T(8,128)S(1)}, f32[21,22,3]{2,0,1:T(8,128)S(1)}, u32[]{:S(2)}, u32[]{:S(2)}) collective-permute-start(f32[21,22,3]{2,0,1:T(8,128)S(1)} %get-tuple-element.219), channel_id=1, source_target_pairs={{0,1},{1,2},{2,3},{3,4},{4,5},{5,6},{6,7},{7,8},{8,9},{9,10},{10,1... | collective-permute-start | bytes 16640 | tf_op jit(solution)/shard_map/ppermute | solution.py:22
  132.4 12.9 %collective-permute-start.15 = (f32[21,22,3]{2,0,1:T(8,128)S(1)}, f32[21,22,3]{2,0,1:T(8,128)S(1)}, u32[]{:S(2)}, u32[]{:S(2)}) collective-permute-start(f32[21,22,3]{2,0,1:T(8,128)S(1)} %get-tuple-element.220), channel_id=1, source_target_pairs={{1,0},{2,1},{3,2},{4,3},{5,4},{6,5},{7,6},{8,7},{9,8},{10,9},{11,1... | collective-permute-start | bytes 16640 | tf_op jit(solution)/shard_map/ppermute | solution.py:25
  158.6 98.9 %copy-start.125 = (f32[16,128]{1,0:T(8,128)S(1)}, f32[16,128]{1,0:T(8,128)}, u32[]{:S(2)}) copy-start(f32[16,128]{1,0:T(8,128)} %get-tuple-element.14) | copy-start | bytes 24580
  158.7 98.9 %copy-start.130 = (f32[16,128]{1,0:T(8,128)S(1)}, f32[16,128]{1,0:T(8,128)}, u32[]{:S(2)}) copy-start(f32[16,128]{1,0:T(8,128)} %get-tuple-element.8) | copy-start | bytes 24580
  158.7 98.9 %copy-start.129 = (f32[16,128]{1,0:T(8,128)S(1)}, f32[16,128]{1,0:T(8,128)}, u32[]{:S(2)}) copy-start(f32[16,128]{1,0:T(8,128)} %get-tuple-element.7) | copy-start | bytes 24580
  158.7 98.9 %copy-start.128 = (f32[16,128]{1,0:T(8,128)S(1)}, f32[16,128]{1,0:T(8,128)}, u32[]{:S(2)}) copy-start(f32[16,128]{1,0:T(8,128)} %get-tuple-element.6) | copy-start | bytes 24580
  241.5 16.1 %collective-permute-start.16 = (f32[21,3,128]{2,0,1:T(8,128)S(1)}, f32[21,3,128]{2,0,1:T(8,128)S(1)}, u32[]{:S(2)}, u32[]{:S(2)}) collective-permute-start(f32[21,3,128]{2,0,1:T(8,128)S(1)} %get-tuple-element.232), channel_id=1, source_target_pairs={{0,16},{16,32},{32,48},{48,64},{64,80},{80,96},{96,112},{112,128},... | collective-permute-start | bytes 96776 | tf_op jit(solution)/shard_map/ppermute | solution.py:22
  243.5 14.2 %collective-permute-start.17 = (f32[21,3,128]{2,0,1:T(8,128)S(1)}, f32[21,3,128]{2,0,1:T(8,128)S(1)}, u32[]{:S(2)}, u32[]{:S(2)}) collective-permute-start(f32[21,3,128]{2,0,1:T(8,128)S(1)} %get-tuple-element.233), channel_id=1, source_target_pairs={{16,0},{32,16},{48,32},{64,48},{80,64},{96,80},{112,96},{128,112},... | collective-permute-start | bytes 96776 | tf_op jit(solution)/shard_map/ppermute | solution.py:25
  257.8 14.9 %collective-permute-start.18 = (f32[21,22,3]{2,0,1:T(8,128)S(1)}, f32[21,22,3]{2,0,1:T(8,128)S(1)}, u32[]{:S(2)}, u32[]{:S(2)}) collective-permute-start(f32[21,22,3]{2,0,1:T(8,128)S(1)} %get-tuple-element.215), channel_id=1, source_target_pairs={{0,1},{1,2},{2,3},{3,4},{4,5},{5,6},{6,7},{7,8},{8,9},{9,10},{10,1... | collective-permute-start | bytes 16640 | tf_op jit(solution)/shard_map/ppermute | solution.py:22
  261.6 14.6 %collective-permute-start.19 = (f32[21,22,3]{2,0,1:T(8,128)S(1)}, f32[21,22,3]{2,0,1:T(8,128)S(1)}, u32[]{:S(2)}, u32[]{:S(2)}) collective-permute-start(f32[21,22,3]{2,0,1:T(8,128)S(1)} %get-tuple-element.216), channel_id=1, source_target_pairs={{1,0},{2,1},{3,2},{4,3},{5,4},{6,5},{7,6},{8,7},{9,8},{10,9},{11,1... | collective-permute-start | bytes 16640 | tf_op jit(solution)/shard_map/ppermute | solution.py:25
  (152 other events, 6748.9 us)
where the time goes:
time: 319 us; the launch traced here: 314 us
  other arithmetic  84.1 us (26%)
  blocking collectives  81.1 us (25%)
  starting transfers between devices  67.7 us (21%)
  waiting for transfers between devices  59.5 us (19%)
  local copies, waits for them, and re-layouts  14.4 us (5%)
  between operations  3.99 us (1%)
  matrix products  3.54 us (1%)
    psum x1, blocking collectives, on_device(): lax.psum(compat_sum, ('rows', 'cols')) / math.sqrt(total_pixels)  81.1 us
    ppermute x10, starting transfers between devices, with_halo(): lax.ppermute(lax.slice_in_dim(block, block.shape[dim] - width, None, axis...  40.5 us
    ppermute x10, waiting for transfers between devices, with_halo(): lax.ppermute(lax.slice_in_dim(block, 0, width, axis=dim), axis, backward)  31.4 us
    ppermute x10, waiting for transfers between devices, with_halo(): lax.ppermute(lax.slice_in_dim(block, block.shape[dim] - width, None, axis...  28.1 us
    ppermute x10, starting transfers between devices, with_halo(): lax.ppermute(lax.slice_in_dim(block, 0, width, axis=dim), axis, backward)  27.2 us
    reduce_sum x16, other arithmetic, pair_terms(): jnp.sum(grad_center * prob_shift + grad_shift * prob_center, axis=0)  16.8 us
    mul x24, other arithmetic, affinity(): spatial_weight(row_step, col_step) * jnp.exp(-distance * factor)  14 us
    sub x1, other arithmetic, softmax_grad(): return prob * (cotangent - jnp.sum(cotangent * prob, axis=0, keepdims=True))  13.9 us
  transfers between devices with their start and end apart: 20, of which 11 were waited for; matrix products, arithmetic and copies ran while one was open for 4% of the time, Pallas kernels for 0%

commit v1 on v0

--- a/solution.py
+++ b/solution.py
@@ -1,8 +1,10 @@
+import functools
 import math
 import jax
 import jax.numpy as jnp
 from jax import lax
 from jax.sharding import PartitionSpec as P
+from jax.lax import psum
 
 ITERS = 2
 THETA_PIXELS = 3.0
@@ -12,6 +14,15 @@
     for col_step in range(-3, 4)
     if row_step != 0 or col_step != 0
 ]
+
+
+def guide_zone(matrix, device_axis, axis_id):
+    for dev_i in (device_axis, axis_id):
+        matrix = psum(matrix, dev_i)
+    return matrix
+
+
+edit_ratios_over_axis = functools.partial(guide_zone, device_axis="rows", axis_id="cols")
 
 
 def with_halo(block, sides, width):
@@ -153,7 +164,7 @@
         coefs = coefs + pair_terms(grad_wide, prob_wide)
     unary_grad = unary_sum + softmax_grad(prob_list[0], cotangent)
     feature_grad = feature_term(coefs, kernel_at(), feat_wide)
-    compat_grad = lax.psum(compat_sum, ("rows", "cols")) / math.sqrt(total_pixels)
+    compat_grad = edit_ratios_over_axis(compat_sum) / math.sqrt(total_pixels)
     return (unary_grad, feature_grad, compat_grad)
 
 

time: 319 us -> 368 us (1.15)
  the two profiles are of different devices: /device:TPU:33 before, /device:TPU:129 now
where the time goes in v1:
time: 368 us; the launch traced here: 363 us
  blocking collectives  108 us (29%)
  starting transfers between devices  89.9 us (24%)
  other arithmetic  84.1 us (23%)
  waiting for transfers between devices  59.1 us (16%)
  local copies, waits for them, and re-layouts  14.4 us (4%)
  between operations  4 us (1%)
    psum x2, blocking collectives, guide_zone(): matrix = psum(matrix, dev_i)  108 us
    ppermute x10, starting transfers between devices, with_halo(): lax.ppermute(lax.slice_in_dim(block, block.shape[dim] - width, None, axis...  51.1 us
    ppermute x10, waiting for transfers between devices, with_halo(): lax.ppermute(lax.slice_in_dim(block, 0, width, axis=dim), axis, backward)  40.4 us
    ppermute x10, starting transfers between devices, with_halo(): lax.ppermute(lax.slice_in_dim(block, 0, width, axis=dim), axis, backward)  38.8 us
    ppermute x10, waiting for transfers between devices, with_halo(): lax.ppermute(lax.slice_in_dim(block, block.shape[dim] - width, None, axis...  18.7 us
    reduce_sum x16, other arithmetic, pair_terms(): jnp.sum(grad_center * prob_shift + grad_shift * prob_center, axis=0)  16.8 us
    mul x24, other arithmetic, affinity(): spatial_weight(row_step, col_step) * jnp.exp(-distance * factor)  14 us
    sub x1, other arithmetic, softmax_grad(): return prob * (cotangent - jnp.sum(cotangent * prob, axis=0, keepdims=True))  13.9 us
  transfers between devices with their start and end apart: 20, of which 11 were waited for; matrix products, arithmetic and copies ran while one was open for 4% of the time, Pallas kernels for 0%

profile of v1, /device:TPU:129, one launch (start us, length us, event | category | flops | bytes accessed | tf_op | source)
XLA Modules:
  0.0 363.2 jit_solution(11681966647966359044)
XLA Ops:
  3.7 3.8 %collective-permute-start.3 = (f32[21,3,128]{2,0,1:T(8,128)S(1)}, f32[21,3,128]{2,0,1:T(8,128)S(1)}, u32[]{:S(2)}, u32[]{:S(2)}) collective-permute-start(f32[21,3,128]{2,0,1:T(8,128)S(1)} %get-tuple-element.238), channel_id=1, source_target_pairs={{0,16},{16,32},{32,48},{48,64},{64,80},{80,96},{96,112},{112,128},... | collective-permute-start | bytes 96776 | tf_op jit(solution)/shard_map/ppermute | solution.py:33
  9.5 3.6 %collective-permute-start = (bf16[64,3,128]{2,1,0:T(4,128)(2,1)S(1)}, bf16[64,3,128]{2,1,0:T(4,128)(2,1)S(1)}, u32[]{:S(2)}, u32[]{:S(2)}) collective-permute-start(bf16[64,3,128]{2,1,0:T(4,128)(2,1)S(1)} %get-tuple-element.229), channel_id=1, source_target_pairs={{0,16},{16,32},{32,48},{48,64},{64,80},{80,96},{96,112},{112,128},... | collective-permute-start | bytes 147464 | tf_op jit(solution)/shard_map/ppermute | solution.py:33
  15.2 4.5 %collective-permute-start.5 = (f32[21,22,3]{2,0,1:T(8,128)S(1)}, f32[21,22,3]{2,0,1:T(8,128)S(1)}, u32[]{:S(2)}, u32[]{:S(2)}) collective-permute-start(f32[21,22,3]{2,0,1:T(8,128)S(1)} %get-tuple-element.227), channel_id=1, source_target_pairs={{0,1},{1,2},{2,3},{3,4},{4,5},{5,6},{6,7},{7,8},{8,9},{9,10},{10,1... | collective-permute-start | bytes 16640 | tf_op jit(solution)/shard_map/ppermute | solution.py:33
  19.8 4.4 %collective-permute-start.7 = (f32[21,22,3]{2,0,1:T(8,128)S(1)}, f32[21,22,3]{2,0,1:T(8,128)S(1)}, u32[]{:S(2)}, u32[]{:S(2)}) collective-permute-start(f32[21,22,3]{2,0,1:T(8,128)S(1)} %get-tuple-element.228), channel_id=1, source_target_pairs={{1,0},{2,1},{3,2},{4,3},{5,4},{6,5},{7,6},{8,7},{9,8},{10,9},{11,1... | collective-permute-start | bytes 16640 | tf_op jit(solution)/shard_map/ppermute | solution.py:36
  24.2 7.0 %collective-permute-done.5 = f32[21,22,3]{2,0,1:T(8,128)S(1)} collective-permute-done((f32[21,22,3]{2,0,1:T(8,128)S(1)}, f32[21,22,3]{2,0,1:T(8,128)S(1)}, u32[]{:S(2)}, u32[]{:S(2)}) %collective-permute-start.5) | collective-permute-done | bytes 5576 | tf_op jit(solution)/shard_map/ppermute | solution.py:33
  37.4 4.3 %collective-permute-start.2 = (bf16[64,22,3]{2,1,0:T(8,128)(2,1)S(1)}, bf16[64,22,3]{2,1,0:T(8,128)(2,1)S(1)}, u32[]{:S(2)}, u32[]{:S(2)}) collective-permute-start(bf16[64,22,3]{2,1,0:T(8,128)(2,1)S(1)} %get-tuple-element.212), channel_id=1, source_target_pairs={{0,1},{1,2},{2,3},{3,4},{4,5},{5,6},{6,7},{7,8},{8,9},{9,10},{10,1... | collective-permute-start | bytes 25352 | tf_op jit(solution)/shard_map/ppermute | solution.py:33
  41.8 15.3 %collective-permute-done.6 = bf16[64,22,3]{2,1,0:T(8,128)(2,1)S(1)} collective-permute-done((bf16[64,22,3]{2,1,0:T(8,128)(2,1)S(1)}, bf16[64,22,3]{2,1,0:T(8,128)(2,1)S(1)}, u32[]{:S(2)}, u32[]{:S(2)}) %collective-permute-start.6) | collective-permute-done | bytes 8480 | tf_op jit(solution)/shard_map/ppermute | solution.py:36
  84.6 5.8 %collective-permute-start.8 = (f32[21,3,128]{2,0,1:T(8,128)S(1)}, f32[21,3,128]{2,0,1:T(8,128)S(1)}, u32[]{:S(2)}, u32[]{:S(2)}) collective-permute-start(f32[21,3,128]{2,0,1:T(8,128)S(1)} %get-tuple-element.236), channel_id=1, source_target_pairs={{0,16},{16,32},{32,48},{48,64},{64,80},{80,96},{96,112},{112,128},... | collective-permute-start | bytes 96776 | tf_op jit(solution)/shard_map/ppermute | solution.py:33
  99.4 5.5 %collective-permute-start.11 = (f32[21,22,3]{2,0,1:T(8,128)S(1)}, f32[21,22,3]{2,0,1:T(8,128)S(1)}, u32[]{:S(2)}, u32[]{:S(2)}) collective-permute-start(f32[21,22,3]{2,0,1:T(8,128)S(1)} %get-tuple-element.224), channel_id=1, source_target_pairs={{1,0},{2,1},{3,2},{4,3},{5,4},{6,5},{7,6},{8,7},{9,8},{10,9},{11,1... | collective-permute-start | bytes 16640 | tf_op jit(solution)/shard_map/ppermute | solution.py:36
  104.9 4.9 %collective-permute-done.10 = f32[21,22,3]{2,0,1:T(8,128)S(1)} collective-permute-done((f32[21,22,3]{2,0,1:T(8,128)S(1)}, f32[21,22,3]{2,0,1:T(8,128)S(1)}, u32[]{:S(2)}, u32[]{:S(2)}) %collective-permute-start.10) | collective-permute-done | bytes 5576 | tf_op jit(solution)/shard_map/ppermute | solution.py:33
  109.8 4.0 %collective-permute-done.11 = f32[21,22,3]{2,0,1:T(8,128)S(1)} collective-permute-done((f32[21,22,3]{2,0,1:T(8,128)S(1)}, f32[21,22,3]{2,0,1:T(8,128)S(1)}, u32[]{:S(2)}, u32[]{:S(2)}) %collective-permute-start.11) | collective-permute-done | bytes 5576 | tf_op jit(solution)/shard_map/ppermute | solution.py:36
  120.9 4.6 %collective-permute-start.12 = (f32[21,3,128]{2,0,1:T(8,128)S(1)}, f32[21,3,128]{2,0,1:T(8,128)S(1)}, u32[]{:S(2)}, u32[]{:S(2)}) collective-permute-start(f32[21,3,128]{2,0,1:T(8,128)S(1)} %get-tuple-element.234), channel_id=1, source_target_pairs={{0,16},{16,32},{32,48},{48,64},{64,80},{80,96},{96,112},{112,128},... | collective-permute-start | bytes 96776 | tf_op jit(solution)/shard_map/ppermute | solution.py:33
  132.8 7.0 %collective-permute-start.15 = (f32[21,22,3]{2,0,1:T(8,128)S(1)}, f32[21,22,3]{2,0,1:T(8,128)S(1)}, u32[]{:S(2)}, u32[]{:S(2)}) collective-permute-start(f32[21,22,3]{2,0,1:T(8,128)S(1)} %get-tuple-element.220), channel_id=1, source_target_pairs={{1,0},{2,1},{3,2},{4,3},{5,4},{6,5},{7,6},{8,7},{9,8},{10,9},{11,1... | collective-permute-start | bytes 16640 | tf_op jit(solution)/shard_map/ppermute | solution.py:36
  143.1 5.8 %collective-permute-done.15 = f32[21,22,3]{2,0,1:T(8,128)S(1)} collective-permute-done((f32[21,22,3]{2,0,1:T(8,128)S(1)}, f32[21,22,3]{2,0,1:T(8,128)S(1)}, u32[]{:S(2)}, u32[]{:S(2)}) %collective-permute-start.15) | collective-permute-done | bytes 5576 | tf_op jit(solution)/shard_map/ppermute | solution.py:36
  155.7 4.4 %add_reduce_fusion.48 = (f32[16,128]{1,0:T(8,128)}, f32[16,128]{1,0:T(8,128)}, f32[16,128]{1,0:T(8,128)}, f32[16,128]{1,0:T(8,128)}, f32[16,128]{1,0:T(8,128)}, ...) fusion(f32[21,16,128]{2,0,1:T(8,128)S(1)} %fusion.11, ...), kind=kLoop, calls=%fused_computation.349 | loop fusion | flops 5830656 | bytes 9657344 | tf_op jit(solution)/shard_map/reduce_sum | solution.py:88
  163.4 48.9 %psum.14 = f32[21,21]{1,0:T(8,128)S(1)} all-reduce(f32[21,21]{1,0:T(8,128)S(1)} %fusion.15), channel_id=1, replica_groups=mesh['rows'=16,'cols'=16] {'rows'}, use_global_device_ids=true, to_apply=%region_153.0 | all-reduce | flops 441 | bytes 3528 | tf_op jit(solution)/shard_map/psum | solution.py:21
  212.3 59.3 %psum.15 = f32[21,21]{1,0:T(8,128)S(1)} all-reduce(f32[21,21]{1,0:T(8,128)S(1)} %psum.14), channel_id=1, replica_groups=mesh['rows'=16,'cols'=16] {'cols'}, use_global_device_ids=true, to_apply=%region_154.0 | all-reduce | flops 441 | bytes 3528 | tf_op jit(solution)/shard_map/psum | solution.py:21
  272.2 17.1 %collective-permute-start.16 = (f32[21,3,128]{2,0,1:T(8,128)S(1)}, f32[21,3,128]{2,0,1:T(8,128)S(1)}, u32[]{:S(2)}, u32[]{:S(2)}) collective-permute-start(f32[21,3,128]{2,0,1:T(8,128)S(1)} %get-tuple-element.232), channel_id=1, source_target_pairs={{0,16},{16,32},{32,48},{48,64},{64,80},{80,96},{96,112},{112,128},... | collective-permute-start | bytes 96776 | tf_op jit(solution)/shard_map/ppermute | solution.py:33
  289.3 4.6 %collective-permute-start.17 = (f32[21,3,128]{2,0,1:T(8,128)S(1)}, f32[21,3,128]{2,0,1:T(8,128)S(1)}, u32[]{:S(2)}, u32[]{:S(2)}) collective-permute-start(f32[21,3,128]{2,0,1:T(8,128)S(1)} %get-tuple-element.233), channel_id=1, source_target_pairs={{16,0},{32,16},{48,32},{64,48},{80,64},{96,80},{112,96},{128,112},... | collective-permute-start | bytes 96776 | tf_op jit(solution)/shard_map/ppermute | solution.py:36
  307.8 7.2 %collective-permute-start.19 = (f32[21,22,3]{2,0,1:T(8,128)S(1)}, f32[21,22,3]{2,0,1:T(8,128)S(1)}, u32[]{:S(2)}, u32[]{:S(2)}) collective-permute-start(f32[21,22,3]{2,0,1:T(8,128)S(1)} %get-tuple-element.216), channel_id=1, source_target_pairs={{1,0},{2,1},{3,2},{4,3},{5,4},{6,5},{7,6},{8,7},{9,8},{10,9},{11,1... | collective-permute-start | bytes 16640 | tf_op jit(solution)/shard_map/ppermute | solution.py:36
  315.3 4.3 %collective-permute-done.18 = f32[21,22,3]{2,0,1:T(8,128)S(1)} collective-permute-done((f32[21,22,3]{2,0,1:T(8,128)S(1)}, f32[21,22,3]{2,0,1:T(8,128)S(1)}, u32[]{:S(2)}, u32[]{:S(2)}) %collective-permute-start.18) | collective-permute-done | bytes 5576 | tf_op jit(solution)/shard_map/ppermute | solution.py:33
  319.6 5.6 %collective-permute-done.19 = f32[21,22,3]{2,0,1:T(8,128)S(1)} collective-permute-done((f32[21,22,3]{2,0,1:T(8,128)S(1)}, f32[21,22,3]{2,0,1:T(8,128)S(1)}, u32[]{:S(2)}, u32[]{:S(2)}) %collective-permute-start.19) | collective-permute-done | bytes 5576 | tf_op jit(solution)/shard_map/ppermute | solution.py:36
  339.9 13.9 %fusion.7 = f32[21,16,128]{2,0,1:T(8,128)S(1)} fusion(f32[21,16,128]{2,0,1:T(8,128)S(1)} %copy-done.10, f32[16,128]{1,0:T(8,128)} %fusion.19, f32[21,16,128]{2,1,0:T(8,128)} %param.7, f32[21,16,128]{2,0,1:T(8,128)} %copy-done.11, f32[16,128]{1,0:T(8,128)} %get-tuple-element.242, f32[16,128]{1,0:T(8,128)S(1)} %copy-done.13, f32[16,128]{1,0:T(8,128)S(1)} %reduce_max.27, ...), kind=kOutput, calls=%fused_computation.55 | output fusion | flops 9205780 | bytes 18972672 | tf_op jit(solution)/shard_map/sub | solution.py:120
  354.9 8.3 %multiply_add_fusion = f32[64,16,128]{2,1,0:T(8,128)} fusion(bf16[64,16,128]{2,1,0:T(8,128)(2,1)S(1)} %copy-done.6, bf16[64,3,128]{2,1,0:T(4,128)(2,1)S(1)} %collective-permute-done, f32[16,128]{1,0:T(8,128)} %get-tuple-element.162, f32[16,128]{1,0:T(8,128)} %get-tuple-element.163, f32[16,128]{1,0:T(8,128)} %get-tuple-element.164, ...), kind=kLoop, calls=%fused_computation.80 | loop fusion | flops 26345472 | bytes 13025280 | tf_op jit(solution)/shard_map/add | solution.py:103
  (517 shorter events, 105.2 us)
Async XLA Ops:
  3.7 11.4 %collective-permute-start.3 = (f32[21,3,128]{2,0,1:T(8,128)S(1)}, f32[21,3,128]{2,0,1:T(8,128)S(1)}, u32[]{:S(2)}, u32[]{:S(2)}) collective-permute-start(f32[21,3,128]{2,0,1:T(8,128)S(1)} %get-tuple-element.238), channel_id=1, source_target_pairs={{0,16},{16,32},{32,48},{48,64},{64,80},{80,96},{96,112},{112,128},... | collective-permute-start | bytes 96776 | tf_op jit(solution)/shard_map/ppermute | solution.py:33
  7.5 7.6 %collective-permute-start.4 = (f32[21,3,128]{2,0,1:T(8,128)S(1)}, f32[21,3,128]{2,0,1:T(8,128)S(1)}, u32[]{:S(2)}, u32[]{:S(2)}) collective-permute-start(f32[21,3,128]{2,0,1:T(8,128)S(1)} %get-tuple-element.239), channel_id=1, source_target_pairs={{16,0},{32,16},{48,32},{64,48},{80,64},{96,80},{112,96},{128,112},... | collective-permute-start | bytes 96776 | tf_op jit(solution)/shard_map/ppermute | solution.py:36
  9.5 25.0 %collective-permute-start = (bf16[64,3,128]{2,1,0:T(4,128)(2,1)S(1)}, bf16[64,3,128]{2,1,0:T(4,128)(2,1)S(1)}, u32[]{:S(2)}, u32[]{:S(2)}) collective-permute-start(bf16[64,3,128]{2,1,0:T(4,128)(2,1)S(1)} %get-tuple-element.229), channel_id=1, source_target_pairs={{0,16},{16,32},{32,48},{48,64},{64,80},{80,96},{96,112},{112,128},... | collective-permute-start | bytes 147464 | tf_op jit(solution)/shard_map/ppermute | solution.py:33
  13.1 21.4 %collective-permute-start.1 = (bf16[64,3,128]{2,1,0:T(4,128)(2,1)S(1)}, bf16[64,3,128]{2,1,0:T(4,128)(2,1)S(1)}, u32[]{:S(2)}, u32[]{:S(2)}) collective-permute-start(bf16[64,3,128]{2,1,0:T(4,128)(2,1)S(1)} %get-tuple-element.230), channel_id=1, source_target_pairs={{16,0},{32,16},{48,32},{64,48},{80,64},{96,80},{112,96},{128,112},... | collective-permute-start | bytes 147464 | tf_op jit(solution)/shard_map/ppermute | solution.py:36
  15.2 15.9 %collective-permute-start.5 = (f32[21,22,3]{2,0,1:T(8,128)S(1)}, f32[21,22,3]{2,0,1:T(8,128)S(1)}, u32[]{:S(2)}, u32[]{:S(2)}) collective-permute-start(f32[21,22,3]{2,0,1:T(8,128)S(1)} %get-tuple-element.227), channel_id=1, source_target_pairs={{0,1},{1,2},{2,3},{3,4},{4,5},{5,6},{6,7},{7,8},{8,9},{9,10},{10,1... | collective-permute-start | bytes 16640 | tf_op jit(solution)/shard_map/ppermute | solution.py:33
  19.8 14.5 %collective-permute-start.7 = (f32[21,22,3]{2,0,1:T(8,128)S(1)}, f32[21,22,3]{2,0,1:T(8,128)S(1)}, u32[]{:S(2)}, u32[]{:S(2)}) collective-permute-start(f32[21,22,3]{2,0,1:T(8,128)S(1)} %get-tuple-element.228), channel_id=1, source_target_pairs={{1,0},{2,1},{3,2},{4,3},{5,4},{6,5},{7,6},{8,7},{9,8},{10,9},{11,1... | collective-permute-start | bytes 16640 | tf_op jit(solution)/shard_map/ppermute | solution.py:36
  34.9 22.1 %collective-permute-start.6 = (bf16[64,22,3]{2,1,0:T(8,128)(2,1)S(1)}, bf16[64,22,3]{2,1,0:T(8,128)(2,1)S(1)}, u32[]{:S(2)}, u32[]{:S(2)}) collective-permute-start(bf16[64,22,3]{2,1,0:T(8,128)(2,1)S(1)} %get-tuple-element.211), channel_id=1, source_target_pairs={{1,0},{2,1},{3,2},{4,3},{5,4},{6,5},{7,6},{8,7},{9,8},{10,9},{11,1... | collective-permute-start | bytes 25352 | tf_op jit(solution)/shard_map/ppermute | solution.py:36
  37.4 19.6 %collective-permute-start.2 = (bf16[64,22,3]{2,1,0:T(8,128)(2,1)S(1)}, bf16[64,22,3]{2,1,0:T(8,128)(2,1)S(1)}, u32[]{:S(2)}, u32[]{:S(2)}) collective-permute-start(bf16[64,22,3]{2,1,0:T(8,128)(2,1)S(1)} %get-tuple-element.212), channel_id=1, source_target_pairs={{0,1},{1,2},{2,3},{3,4},{4,5},{5,6},{6,7},{7,8},{8,9},{9,10},{10,1... | collective-permute-start | bytes 25352 | tf_op jit(solution)/shard_map/ppermute | solution.py:33
  84.6 7.7 %collective-permute-start.8 = (f32[21,3,128]{2,0,1:T(8,128)S(1)}, f32[21,3,128]{2,0,1:T(8,128)S(1)}, u32[]{:S(2)}, u32[]{:S(2)}) collective-permute-start(f32[21,3,128]{2,0,1:T(8,128)S(1)} %get-tuple-element.236), channel_id=1, source_target_pairs={{0,16},{16,32},{32,48},{48,64},{64,80},{80,96},{96,112},{112,128},... | collective-permute-start | bytes 96776 | tf_op jit(solution)/shard_map/ppermute | solution.py:33
  90.4 5.3 %collective-permute-start.9 = (f32[21,3,128]{2,0,1:T(8,128)S(1)}, f32[21,3,128]{2,0,1:T(8,128)S(1)}, u32[]{:S(2)}, u32[]{:S(2)}) collective-permute-start(f32[21,3,128]{2,0,1:T(8,128)S(1)} %get-tuple-element.237), channel_id=1, source_target_pairs={{16,0},{32,16},{48,32},{64,48},{80,64},{96,80},{112,96},{128,112},... | collective-permute-start | bytes 96776 | tf_op jit(solution)/shard_map/ppermute | solution.py:36
  95.8 14.0 %collective-permute-start.10 = (f32[21,22,3]{2,0,1:T(8,128)S(1)}, f32[21,22,3]{2,0,1:T(8,128)S(1)}, u32[]{:S(2)}, u32[]{:S(2)}) collective-permute-start(f32[21,22,3]{2,0,1:T(8,128)S(1)} %get-tuple-element.223), channel_id=1, source_target_pairs={{0,1},{1,2},{2,3},{3,4},{4,5},{5,6},{6,7},{7,8},{8,9},{9,10},{10,1... | collective-permute-start | bytes 16640 | tf_op jit(solution)/shard_map/ppermute | solution.py:33
  99.4 14.4 %collective-permute-start.11 = (f32[21,22,3]{2,0,1:T(8,128)S(1)}, f32[21,22,3]{2,0,1:T(8,128)S(1)}, u32[]{:S(2)}, u32[]{:S(2)}) collective-permute-start(f32[21,22,3]{2,0,1:T(8,128)S(1)} %get-tuple-element.224), channel_id=1, source_target_pairs={{1,0},{2,1},{3,2},{4,3},{5,4},{6,5},{7,6},{8,7},{9,8},{10,9},{11,1... | collective-permute-start | bytes 16640 | tf_op jit(solution)/shard_map/ppermute | solution.py:36
  120.9 6.5 %collective-permute-start.12 = (f32[21,3,128]{2,0,1:T(8,128)S(1)}, f32[21,3,128]{2,0,1:T(8,128)S(1)}, u32[]{:S(2)}, u32[]{:S(2)}) collective-permute-start(f32[21,3,128]{2,0,1:T(8,128)S(1)} %get-tuple-element.234), channel_id=1, source_target_pairs={{0,16},{16,32},{32,48},{48,64},{64,80},{80,96},{96,112},{112,128},... | collective-permute-start | bytes 96776 | tf_op jit(solution)/shard_map/ppermute | solution.py:33
  125.5 5.3 %collective-permute-start.13 = (f32[21,3,128]{2,0,1:T(8,128)S(1)}, f32[21,3,128]{2,0,1:T(8,128)S(1)}, u32[]{:S(2)}, u32[]{:S(2)}) collective-permute-start(f32[21,3,128]{2,0,1:T(8,128)S(1)} %get-tuple-element.235), channel_id=1, source_target_pairs={{16,0},{32,16},{48,32},{64,48},{80,64},{96,80},{112,96},{128,112},... | collective-permute-start | bytes 96776 | tf_op jit(solution)/shard_map/ppermute | solution.py:36
  130.9 12.2 %collective-permute-start.14 = (f32[21,22,3]{2,0,1:T(8,128)S(1)}, f32[21,22,3]{2,0,1:T(8,128)S(1)}, u32[]{:S(2)}, u32[]{:S(2)}) collective-permute-start(f32[21,22,3]{2,0,1:T(8,128)S(1)} %get-tuple-element.219), channel_id=1, source_target_pairs={{0,1},{1,2},{2,3},{3,4},{4,5},{5,6},{6,7},{7,8},{8,9},{9,10},{10,1... | collective-permute-start | bytes 16640 | tf_op jit(solution)/shard_map/ppermute | solution.py:33
  132.8 16.0 %collective-permute-start.15 = (f32[21,22,3]{2,0,1:T(8,128)S(1)}, f32[21,22,3]{2,0,1:T(8,128)S(1)}, u32[]{:S(2)}, u32[]{:S(2)}) collective-permute-start(f32[21,22,3]{2,0,1:T(8,128)S(1)} %get-tuple-element.220), channel_id=1, source_target_pairs={{1,0},{2,1},{3,2},{4,3},{5,4},{6,5},{7,6},{8,7},{9,8},{10,9},{11,1... | collective-permute-start | bytes 16640 | tf_op jit(solution)/shard_map/ppermute | solution.py:36
  162.2 143.3 %copy-start.125 = (f32[16,128]{1,0:T(8,128)S(1)}, f32[16,128]{1,0:T(8,128)}, u32[]{:S(2)}) copy-start(f32[16,128]{1,0:T(8,128)} %get-tuple-element.14) | copy-start | bytes 24580
  162.3 143.4 %copy-start.130 = (f32[16,128]{1,0:T(8,128)S(1)}, f32[16,128]{1,0:T(8,128)}, u32[]{:S(2)}) copy-start(f32[16,128]{1,0:T(8,128)} %get-tuple-element.8) | copy-start | bytes 24580
  162.3 143.4 %copy-start.129 = (f32[16,128]{1,0:T(8,128)S(1)}, f32[16,128]{1,0:T(8,128)}, u32[]{:S(2)}) copy-start(f32[16,128]{1,0:T(8,128)} %get-tuple-element.7) | copy-start | bytes 24580
  162.3 143.4 %copy-start.128 = (f32[16,128]{1,0:T(8,128)S(1)}, f32[16,128]{1,0:T(8,128)}, u32[]{:S(2)}) copy-start(f32[16,128]{1,0:T(8,128)} %get-tuple-element.6) | copy-start | bytes 24580
  272.2 33.5 %collective-permute-start.16 = (f32[21,3,128]{2,0,1:T(8,128)S(1)}, f32[21,3,128]{2,0,1:T(8,128)S(1)}, u32[]{:S(2)}, u32[]{:S(2)}) collective-permute-start(f32[21,3,128]{2,0,1:T(8,128)S(1)} %get-tuple-element.232), channel_id=1, source_target_pairs={{0,16},{16,32},{32,48},{48,64},{64,80},{80,96},{96,112},{112,128},... | collective-permute-start | bytes 96776 | tf_op jit(solution)/shard_map/ppermute | solution.py:33
  289.3 16.4 %collective-permute-start.17 = (f32[21,3,128]{2,0,1:T(8,128)S(1)}, f32[21,3,128]{2,0,1:T(8,128)S(1)}, u32[]{:S(2)}, u32[]{:S(2)}) collective-permute-start(f32[21,3,128]{2,0,1:T(8,128)S(1)} %get-tuple-element.233), channel_id=1, source_target_pairs={{16,0},{32,16},{48,32},{64,48},{80,64},{96,80},{112,96},{128,112},... | collective-permute-start | bytes 96776 | tf_op jit(solution)/shard_map/ppermute | solution.py:36
  305.9 13.7 %collective-permute-start.18 = (f32[21,22,3]{2,0,1:T(8,128)S(1)}, f32[21,22,3]{2,0,1:T(8,128)S(1)}, u32[]{:S(2)}, u32[]{:S(2)}) collective-permute-start(f32[21,22,3]{2,0,1:T(8,128)S(1)} %get-tuple-element.215), channel_id=1, source_target_pairs={{0,1},{1,2},{2,3},{3,4},{4,5},{5,6},{6,7},{7,8},{8,9},{9,10},{10,1... | collective-permute-start | bytes 16640 | tf_op jit(solution)/shard_map/ppermute | solution.py:33
  307.8 17.4 %collective-permute-start.19 = (f32[21,22,3]{2,0,1:T(8,128)S(1)}, f32[21,22,3]{2,0,1:T(8,128)S(1)}, u32[]{:S(2)}, u32[]{:S(2)}) collective-permute-start(f32[21,22,3]{2,0,1:T(8,128)S(1)} %get-tuple-element.216), channel_id=1, source_target_pairs={{1,0},{2,1},{3,2},{4,3},{5,4},{6,5},{7,6},{8,7},{9,8},{10,9},{11,1... | collective-permute-start | bytes 16640 | tf_op jit(solution)/shard_map/ppermute | solution.py:36
  (152 other events, 8043.2 us)
